TPU v7x, 128 devices: a whole 4x4x4 slice. The times are simulated.
128 devices in a mesh: section: 8 (over x, core), expert: 16 (over z, y).
Axes of the slice: x: 4, y: 4, z: 4, core: 2. Of those that a mesh axis runs over, the one named last changes fastest.
Arguments:
- inputs: bfloat16 [8, 2, 1024, 2048], P('section', None, 'expert'), may hold values from -6 to 6
- routes: int32 [8, 2, 1024, 10], P('section', None, 'expert'), may hold values from 0 to 15, all different within a row; in each aligned block of 64 rows (0 to 63, 64 to 127, ..., all dimensions but the last counted through in order) at most 48 rows name the same one
- gates: float32 [8, 2, 1024, 10], P('section', None, 'expert'), may hold values from 0.1 to 0.6
- cot_early: bfloat16 [8, 1024, 2048], P('section', 'expert'), may hold values from -6 to 6
- head_grad: bfloat16 [1024, 2048], P('expert'), may hold values from -6 to 6
- w_gate: bfloat16 [8, 16, 2048, 512], P('section', 'expert'), may hold values from -0.125 to 0.125
- w_up: bfloat16 [8, 16, 2048, 512], P('section', 'expert'), may hold values from -0.125 to 0.125
- w_down: bfloat16 [8, 16, 512, 2048], P('section', 'expert'), may hold values from -0.25 to 0.25
Outputs:
- grad_early: bfloat16 [8, 1024, 2048], P('section', 'expert')
- grad_late: bfloat16 [8, 1024, 2048], P('section', 'expert')
- grad_gate: bfloat16 [8, 16, 2048, 512], P('section', 'expert')
- grad_up: bfloat16 [8, 16, 2048, 512], P('section', 'expert')
- grad_down: bfloat16 [8, 16, 512, 2048], P('section', 'expert')
Inputs may be any that keep to these rules, and one draw needn't show every extreme that they name: `routes`: each row names 10 different experts. In each aligned block of 64 rows (one device's tokens of one micro-batch at one section) no expert is named by more than 48 rows, a bound that some block reaches.
All inputs are finite; a program needn't handle non-finite values.
Results may differ from a plain program's by a relative error of at most 0.008.
Values may be sent and summed in bfloat16 or wider, within the bound.
A program may use at most 128 MiB of HBM per device.

v0:
```python
import functools

import jax
import jax.numpy as jnp
from jax import lax
from jax.experimental import pallas as pl
from jax.experimental.pallas import tpu as pltpu
from jax.sharding import PartitionSpec as P

F32 = jnp.float32
BF16 = jnp.bfloat16
MESH = pl.DeviceIdType.MESH

D = 2048
FF = 512
TOPK = 10
OWNERS = 16
SIDE = 4
ROWS = 16
CHUNKS = 4
STEPS = 2 * CHUNKS
WIDE = D + 128
HALF = D // 2
QUART = D // 4
COT_CUT = 1024
ALL_ROWS = OWNERS * ROWS
NT = (((1,), (1,)), ((), ()))
TN = (((0,), (0,)), ((), ()))


def kernel(
    inputs, routes, gates, cot_early, head_grad, w_gate, w_up, w_down,
    grads, grad_gate, grad_up, grad_down,
    xs, cots, part, land1z, land1y, land2z, land2y, land3, land4, moved, outs, head,
    wg, wu, wd, gate_s, up_s, hid_s, gg_s, gu_s, scaled_s, acc_g, acc_u, acc_d,
    load_sem, ag_send, ag_recv, rs_send, rs_recv, mv_send, mv_recv,
):
    sec = lax.axis_index("section")
    own = lax.axis_index("expert")
    n_sec = lax.axis_size("section")
    z = own // SIDE
    y = own % SIDE
    zp, zm, zo = (z + 1) % SIDE, (z + 3) % SIDE, (z + 2) % SIDE
    yp, ym, yo = (y + 1) % SIDE, (y + 3) % SIDE, (y + 2) % SIDE
    to_zp = (sec, zp * SIDE + y)
    to_zm = (sec, zm * SIDE + y)
    to_yp = (sec, z * SIDE + yp)
    to_ym = (sec, z * SIDE + ym)
    to_below = ((sec + n_sec - 1) % n_sec, own)
    to_above = ((sec + 1) % n_sec, own)

    def at_rows(i):
        return pl.ds(pl.multiple_of(i * ROWS, ROWS), ROWS)

    def blk(buf, k, bz, by, col, width):
        return buf.at[k, bz, at_rows(by), pl.ds(col, width)]

    def zrow(buf, k, bz, col, width):
        return buf.at[k, bz, :, pl.ds(col, width)]

    def ycol(buf, k, by, col, width):
        return buf.at[k, :, at_rows(by), pl.ds(col, width)]

    def remote(src, dst, send, recv, peer):
        return pltpu.make_async_remote_copy(
            src_ref=src, dst_ref=dst, send_sem=send, recv_sem=recv,
            device_id=peer, device_id_type=MESH,
        )

    def ag_copy(which, phase, side, k, arriving):
        buf = cots if which else xs
        width = WIDE if which else D
        cut = COT_CUT if which else HALF
        late = phase >= 2
        on_y = (phase < 2) != bool(which)
        here, plus, minus = (y, yp, ym) if on_y else (z, zp, zm)
        peer = ((to_yp, to_ym) if on_y else (to_zp, to_zm))[side]
        opposite = yo if on_y else zo
        if phase % 2 == 0:
            pos = ((minus, plus)[side]) if arriving else here
            col, wid = 0, width
        else:
            pos = opposite if arriving else (minus, plus)[side]
            col, wid = (0, cut) if side == 0 else (cut, width - cut)
        if late:
            ref = (ycol if on_y else zrow)(buf, k, pos, col, wid)
        elif on_y:
            ref = blk(buf, k, z, pos, col, wid)
        else:
            ref = blk(buf, k, pos, y, col, wid)
        slot = phase * 2 + side
        return remote(ref, ref, ag_send.at[k, which, slot], ag_recv.at[k, which, slot], peer)

    def ag_start(phase, k):
        for which in range(2):
            for side in range(2):
                ag_copy(which, phase, side, k, False).start()

    def ag_wait(phase, k):
        for which in range(2):
            for side in range(2):
                ag_copy(which, phase, side, k, True).wait_recv()

    def rs_copy(phase, part_no, side, k):
        on_y = (part_no == 1) != (phase >= 2)
        base = part_no * HALF
        plus, minus, opposite = (yp, ym, yo) if on_y else (zp, zm, zo)
        peer = ((to_ym, to_yp) if on_y else (to_zm, to_zp))[side]
        if phase % 2 == 0:
            pos = opposite
            col, wid = base + side * QUART, QUART
        else:
            pos = (minus, plus)[side]
            col, wid = base, HALF
        if phase < 2:
            src = (ycol if on_y else zrow)(part, k, pos, col, wid)
            lands = ((land1z, land2z), (land1y, land2y))[part_no]
            dst = lands[phase].at[k, side]
        else:
            src = blk(part, k, z, pos, col, wid) if on_y else blk(part, k, pos, y, col, wid)
            dst = (land3, land4)[phase - 2].at[k, part_no * 2 + side]
        slot = phase * 4 + part_no * 2 + side
        return remote(src, dst, rs_send.at[k, slot], rs_recv.at[k, slot], peer)

    def rs_start(phase, k):
        for part_no in range(2):
            for side in range(2):
                rs_copy(phase, part_no, side, k).start()

    def rs_wait(phase, k):
        for part_no in range(2):
            for side in range(2):
                rs_copy(phase, part_no, side, k).wait_recv()

    def add_to(ref, *others):
        total = ref[...].astype(F32)
        for other in others:
            total = total + other[...].astype(F32)
        ref[...] = total.astype(BF16)

    def move(c):
        return remote(outs.at[c], moved.at[c], mv_send.at[c], mv_recv.at[c], to_below)

    loads = [
        pltpu.make_async_copy(w_gate, wg, load_sem.at[0]),
        pltpu.make_async_copy(w_up, wu, load_sem.at[1]),
        pltpu.make_async_copy(w_down, wd, load_sem.at[2]),
        pltpu.make_async_copy(head_grad, head, load_sem.at[3]),
    ]

    def row_load(k):
        c = k % CHUNKS
        m = k // CHUNKS
        return pltpu.make_async_copy(
            inputs.at[m, pl.ds(c * ROWS, ROWS), :], blk(xs, k, z, y, 0, D), load_sem.at[4 + k]
        )

    def cot_load(c):
        return pltpu.make_async_copy(
            cot_early.at[pl.ds(c * ROWS, ROWS), :], blk(cots, c, z, y, 0, D), load_sem.at[4 + STEPS + c]
        )

    for c in range(CHUNKS):
        row_load(c).start()
        cot_load(c).start()
    for copy in loads:
        copy.start()
    for c in range(CHUNKS, STEPS):
        row_load(c).start()

    barrier = pltpu.get_barrier_semaphore()
    for peer in (to_yp, to_ym, to_zp, to_zm, to_below, to_above):
        pl.semaphore_signal(barrier, inc=1, device_id=peer, device_id_type=MESH)

    lane = lax.broadcasted_iota(jnp.int32, (ROWS, 128), 1)
    for k in range(STEPS):
        m, c = divmod(k, CHUNKS)
        ids = routes[m, c * ROWS:(c + 1) * ROWS, :]
        values = gates[m, c * ROWS:(c + 1) * ROWS, :]
        dense = jnp.zeros((ROWS, 128), F32)
        for choice in range(TOPK):
            hit = ids[:, choice:choice + 1] == (lane & (OWNERS - 1))
            dense = dense + jnp.where(hit, values[:, choice:choice + 1], 0.0)
        high = dense.astype(BF16).astype(F32)
        rest = dense - high
        mid = rest.astype(BF16).astype(F32)
        low = rest - mid
        packed = jnp.where(
            lane < OWNERS, high,
            jnp.where(lane < 2 * OWNERS, mid, jnp.where(lane < 3 * OWNERS, low, 0.0)),
        )
        blk(cots, k, z, y, D, 128)[...] = packed.astype(BF16)

    acc_g[...] = jnp.zeros_like(acc_g)
    acc_u[...] = jnp.zeros_like(acc_u)
    acc_d[...] = jnp.zeros_like(acc_d)
    pick_row = lax.broadcasted_iota(jnp.int32, (128, 128), 0)
    picker = jnp.where(
        ((pick_row & (OWNERS - 1)) == own) & (pick_row < 3 * OWNERS), 1.0, 0.0
    ).astype(BF16)

    for c in range(CHUNKS):
        row_load(c).wait()
        cot_load(c).wait()
    pl.semaphore_wait(barrier, 6)
    ag_start(0, 0)
    for copy in loads:
        copy.wait()
    for c in range(CHUNKS, STEPS):
        row_load(c).wait()
    ag_wait(0, 0)
    ag_start(1, 0)
    ag_wait(1, 0)
    ag_start(2, 0)

    def forward(j):
        rows = xs[j].reshape(ALL_ROWS, D)
        for n in range(2):
            cols = slice(n * 256, (n + 1) * 256)
            gate_s[:, cols] = jnp.dot(rows, wg[:, cols], preferred_element_type=F32)
            up_s[:, cols] = jnp.dot(rows, wu[:, cols], preferred_element_type=F32)

    def backward(j):
        turn = j % 2
        own_gate = jnp.dot(
            cots[j, :, :, D:].reshape(ALL_ROWS, 128), picker, preferred_element_type=F32
        )
        for n in range(D // 128):
            cols = slice(n * 128, (n + 1) * 128)
            tile = cots[j, :, :, cols].reshape(ALL_ROWS, 128).astype(F32)
            scaled_s[turn, :, cols] = (own_gate * tile).astype(BF16)
        for n in range(2):
            cols = slice(n * 256, (n + 1) * 256)
            grad_hidden = lax.dot_general(
                scaled_s[turn], wd[cols, :], NT, preferred_element_type=F32
            )
            gate_value = gate_s[:, cols]
            up_value = up_s[:, cols]
            sigmoid_value = jax.nn.sigmoid(gate_value)
            swished = gate_value * sigmoid_value
            derivative = sigmoid_value * (1.0 + gate_value * (1.0 - sigmoid_value))
            hid_s[turn, :, cols] = (swished * up_value).astype(BF16)
            gg_s[turn, :, cols] = (grad_hidden * up_value * derivative).astype(BF16)
            gu_s[turn, :, cols] = (grad_hidden * swished).astype(BF16)
        for n in range(D // 256):
            cols = slice(n * 256, (n + 1) * 256)
            back = lax.dot_general(gg_s[turn], wg[cols, :], NT, preferred_element_type=F32)
            back = back + lax.dot_general(gu_s[turn], wu[cols, :], NT, preferred_element_type=F32)
            part[j, :, :, cols] = back.astype(BF16).reshape(SIDE, SIDE * ROWS, 256)

    def grow_up_gate(r):
        turn = r % 2
        for n in range(D // 256):
            cols = slice(n * 256, (n + 1) * 256)
            rows = xs[r, :, :, cols].reshape(ALL_ROWS, 256)
            acc_g[cols, :] += lax.dot_general(rows, gg_s[turn], TN, preferred_element_type=F32)
            acc_u[cols, :] += lax.dot_general(rows, gu_s[turn], TN, preferred_element_type=F32)

    def grow_down(r):
        turn = r % 2
        for n in range(D // 256):
            cols = slice(n * 256, (n + 1) * 256)
            acc_d[:, cols] += lax.dot_general(
                hid_s[turn], scaled_s[turn, :, cols], TN, preferred_element_type=F32
            )

    @pl.loop(0, STEPS + 2)
    def _(t):
        k, j, r, n = t, t - 1, t - 2, t + 1
        gathering = k < STEPS
        coming = n < STEPS
        working = (t >= 1) & (j < STEPS)
        reducing = t >= 2

        @pl.when(reducing)
        def _():
            rs_wait(0, r)
            add_to(zrow(part, r, zm, 0, QUART), land1z.at[r, 0])
            add_to(zrow(part, r, zp, QUART, QUART), land1z.at[r, 1])
            add_to(ycol(part, r, ym, HALF, QUART), land1y.at[r, 0])
            add_to(ycol(part, r, yp, HALF + QUART, QUART), land1y.at[r, 1])
            rs_start(1, r)

        @pl.when(working)
        def _():
            forward(j)

        @pl.when(coming & (n >= CHUNKS))
        def _():
            c = n - CHUNKS
            move(c).wait_recv()
            top = sec == n_sec - 1
            value = jnp.where(top, head[at_rows(c), :], moved[c])
            blk(cots, n, z, y, 0, D)[...] = value

        @pl.when(coming)
        def _():
            ag_start(0, n)

        @pl.when(working)
        def _():
            backward(j)
            rs_start(0, j)

        @pl.when(gathering)
        def _():
            ag_wait(2, k)
            ag_start(3, k)

        @pl.when(reducing)
        def _():
            rs_wait(1, r)
            add_to(zrow(part, r, z, 0, HALF), land2z.at[r, 0], land2z.at[r, 1])
            add_to(ycol(part, r, y, HALF, HALF), land2y.at[r, 0], land2y.at[r, 1])
            rs_start(2, r)
            grow_up_gate(r)

        @pl.when(coming)
        def _():
            ag_wait(0, n)
            ag_start(1, n)

        @pl.when(reducing)
        def _():
            rs_wait(2, r)
            add_to(blk(part, r, z, ym, 0, QUART), land3.at[r, 0])
            add_to(blk(part, r, z, yp, QUART, QUART), land3.at[r, 1])
            add_to(blk(part, r, zm, y, HALF, QUART), land3.at[r, 2])
            add_to(blk(part, r, zp, y, HALF + QUART, QUART), land3.at[r, 3])
            rs_start(3, r)
            grow_down(r)

        @pl.when(coming)
        def _():
            ag_wait(1, n)
            ag_start(2, n)

        @pl.when(reducing)
        def _():
            rs_wait(3, r)
            for part_no in range(2):
                base = part_no * HALF
                total = blk(cots, r, z, y, base, HALF)[...].astype(F32)
                total = total + blk(part, r, z, y, base, HALF)[...].astype(F32)
                total = total + land4[r, part_no * 2].astype(F32)
                total = total + land4[r, part_no * 2 + 1].astype(F32)
                outs[r, :, base:base + HALF] = total.astype(BF16)

            @pl.when(r < CHUNKS)
            def _():
                move(r).start()

        @pl.when(gathering)
        def _():
            ag_wait(3, k)

    wg[...] = acc_g[...].astype(BF16)
    store_g = pltpu.make_async_copy(wg, grad_gate, load_sem.at[0])
    store_g.start()
    wu[...] = acc_u[...].astype(BF16)
    store_u = pltpu.make_async_copy(wu, grad_up, load_sem.at[1])
    store_u.start()
    wd[...] = acc_d[...].astype(BF16)
    store_d = pltpu.make_async_copy(wd, grad_down, load_sem.at[2])
    store_d.start()
    store_o = pltpu.make_async_copy(outs, grads, load_sem.at[3])
    store_o.start()

    @pl.loop(0, STEPS)
    def _(k):
        for phase in range(4):
            for which in range(2):
                for side in range(2):
                    ag_copy(which, phase, side, k, False).wait_send()
                    rs_copy(phase, which, side, k).wait_send()

    @pl.loop(0, CHUNKS)
    def _(c):
        move(c).wait_send()

    for copy in (store_g, store_u, store_d, store_o):
        copy.wait()


def on_device(inputs, routes, gates, cot_early, head_grad, w_gate, w_up, w_down):
    hbm = pl.BlockSpec(memory_space=pl.ANY)
    vmem = pl.BlockSpec(memory_space=pltpu.VMEM)
    shape = jax.ShapeDtypeStruct
    block = SIDE * ROWS
    grads, grad_gate, grad_up, grad_down = pl.pallas_call(
        kernel,
        out_shape=(
            shape((STEPS, ROWS, D), BF16),
            shape((D, FF), BF16),
            shape((D, FF), BF16),
            shape((FF, D), BF16),
        ),
        in_specs=[hbm, vmem, vmem, hbm, hbm, hbm, hbm, hbm],
        out_specs=[hbm] * 4,
        scratch_shapes=[
            pltpu.VMEM((STEPS, SIDE, block, D), BF16),
            pltpu.VMEM((STEPS, SIDE, block, WIDE), BF16),
            pltpu.VMEM((STEPS, SIDE, block, D), BF16),
            pltpu.VMEM((STEPS, 2, block, QUART), BF16),
            pltpu.VMEM((STEPS, 2, SIDE, ROWS, QUART), BF16),
            pltpu.VMEM((STEPS, 2, block, HALF), BF16),
            pltpu.VMEM((STEPS, 2, SIDE, ROWS, HALF), BF16),
            pltpu.VMEM((STEPS, 4, ROWS, QUART), BF16),
            pltpu.VMEM((STEPS, 4, ROWS, HALF), BF16),
            pltpu.VMEM((CHUNKS, ROWS, D), BF16),
            pltpu.VMEM((STEPS, ROWS, D), BF16),
            pltpu.VMEM((CHUNKS * ROWS, D), BF16),
            pltpu.VMEM((D, FF), BF16),
            pltpu.VMEM((D, FF), BF16),
            pltpu.VMEM((FF, D), BF16),
            pltpu.VMEM((ALL_ROWS, FF), F32),
            pltpu.VMEM((ALL_ROWS, FF), F32),
            pltpu.VMEM((2, ALL_ROWS, FF), BF16),
            pltpu.VMEM((2, ALL_ROWS, FF), BF16),
            pltpu.VMEM((2, ALL_ROWS, FF), BF16),
            pltpu.VMEM((2, ALL_ROWS, D), BF16),
            pltpu.VMEM((D, FF), F32),
            pltpu.VMEM((D, FF), F32),
            pltpu.VMEM((FF, D), F32),
            pltpu.SemaphoreType.DMA((4 + STEPS + CHUNKS,)),
            pltpu.SemaphoreType.DMA((STEPS, 2, 8)),
            pltpu.SemaphoreType.DMA((STEPS, 2, 8)),
            pltpu.SemaphoreType.DMA((STEPS, 16)),
            pltpu.SemaphoreType.DMA((STEPS, 16)),
            pltpu.SemaphoreType.DMA((CHUNKS,)),
            pltpu.SemaphoreType.DMA((CHUNKS,)),
        ],
        compiler_params=pltpu.CompilerParams(
            collective_id=0, has_side_effects=True, vmem_limit_bytes=67043328
        ),
        cost_estimate=pl.CostEstimate(
            flops=16 * 2 * 1024 * D * FF, bytes_accessed=16 << 20, transcendentals=2 * 1024 * FF
        ),
    )(inputs[0], routes[0], gates[0], cot_early[0], head_grad, w_gate[0, 0], w_up[0, 0], w_down[0, 0])
    tokens = CHUNKS * ROWS
    grads = grads.reshape(2, 1, tokens, D)
    return grads[0], grads[1], grad_gate[None, None], grad_up[None, None], grad_down[None, None]


def solution(mesh):
    in_specs = (
        P("section", None, "expert", None),
        P("section", None, "expert", None),
        P("section", None, "expert", None),
        P("section", "expert", None),
        P("expert", None),
        P("section", "expert", None, None),
        P("section", "expert", None, None),
        P("section", "expert", None, None),
    )
    out_specs = (
        P("section", "expert", None),
        P("section", "expert", None),
        P("section", "expert", None, None),
        P("section", "expert", None, None),
        P("section", "expert", None, None),
    )
    return jax.shard_map(
        on_device, mesh=mesh, in_specs=in_specs, out_specs=out_specs, check_vma=False
    )
```

profile of v0, /device:TPU:0, one launch (start us, length us, event | category | flops | bytes accessed | tf_op | source)
XLA Modules:
  0.0 193.5 jit_solution(13434888652881813919)
XLA Ops:
  0.6 1.4 copy.13
  2.1 1.4 copy.14
  3.5 181.3 %shard_map.119 = (bf16[8,16,2048]{2,1,0:T(8,128)(2,1)}, bf16[2048,512]{1,0:T(8,128)(2,1)}, bf16[2048,512]{1,0:T(8,128)(2,1)}, bf16[512,2048]{1,0:T(8,128)(2,1)}) custom-call(bf16[2,64,2048]{2,1,0:T(8,128)(2,1)} %bitcast.22, s32[2,64,10]{2,1,0:T(8,128)} %bitcast.17, f32[2,64,10]{2,1,0:T(8,128)} %bitcast.18, bf16[64,2048]{1,0:T(8,128)(2,1)} %bitcast.23, ...), custom_call_target="tpu_custom_call" | custom-call | flops 34359738368 | bytes 16777216 | tf_op jit(solution)/shard_map/pallas_call | solution.py:390
  184.8 1.9 fusion
  186.7 0.0 copy-start.1
  186.7 3.2 %copy.18 = bf16[1,1,2048,512]{3,2,1,0:T(8,128)(2,1)} copy(bf16[1,1,2048,512]{3,2,1,0:T(8,128)(2,1)} %bitcast.14) | data formatting | bytes 4194304
  189.9 0.0 copy-done.1
  189.9 0.0 copy-start
  189.9 1.3 copy.19
  191.2 1.0 copy-done
  192.2 1.3 copy.20
Async XLA Ops:
  186.7 3.2 %copy-start.1 = (bf16[2048,512]{1,0:T(8,128)(2,1)S(1)}, bf16[2048,512]{1,0:T(8,128)(2,1)}, u32[]{:S(2)}) copy-start(bf16[2048,512]{1,0:T(8,128)(2,1)} %get-tuple-element.11) | copy-start | bytes 6291460
  189.9 2.3 %copy-start = (bf16[512,2048]{1,0:T(8,128)(2,1)S(1)}, bf16[512,2048]{1,0:T(8,128)(2,1)}, u32[]{:S(2)}) copy-start(bf16[512,2048]{1,0:T(8,128)(2,1)} %get-tuple-element.12) | copy-start | bytes 6291460
where the time goes:
time: 195 us; the launch traced here: 194 us
  Pallas kernels  181 us (93%)
  local copies, waits for them, and re-layouts  11.6 us (6%)
    pallas_call x1, Pallas kernels, on_device(): pl.pallas_call(kernel, out_shape=(shape((STEPS, ROWS, D), BF16), shape((D...  181 us
    unnamed x9, local copies, waits for them, and re-layouts  9.71 us

commit v1 on v0

--- a/solution.py
+++ b/solution.py
@@ -26,6 +26,30 @@
 ALL_ROWS = OWNERS * ROWS
 NT = (((1,), (1,)), ((), ()))
 TN = (((0,), (0,)), ((), ()))
+HEAD = (("P1", 0), ("P1", 1), ("P1", 2), ("P2", 0), ("P1", 3), ("P2", 1), ("P2", 2), ("P3", 0), ("P2", 3),
+        ("P3", 1), ("P4", 0), ("P3", 2), ("P4", 1),)
+AFTER = {
+    (0, "H"): (("P3", 3), ("P4", 2),),
+    (1, "W"): (("R1", 0), ("P4", 3),),
+    (2, "G"): (("R1", 1), ("R2", 0),),
+    (2, "W"): (("R1", 2),),
+    (3, "F"): (("R2", 1),),
+    (3, "G"): (("R3", 0),),
+    (3, "H"): (("R1", 3), ("R2", 2),),
+    (3, "W"): (("R4", 0), ("R3", 1), ("R2", 3), ("R3", 2), ("M", 0), ("R4", 1), ("P1", 4), ("R3", 3), ("R4",
+        2), ("M", 1), ("P2", 4), ("R4", 3), ("M", 2), ("P1", 5), ("P3", 4), ("M", 3), ("P2", 5), ("P1", 6),
+        ("P1", 7), ("P4", 4), ("P2", 6), ("P3", 5), ("P2", 7),),
+    (4, "H"): (("P3", 6),),
+    (4, "W"): (("P4", 5), ("P3", 7), ("P4", 6),),
+    (5, "W"): (("R1", 4), ("P4", 7),),
+    (6, "G"): (("R1", 5), ("R2", 4),),
+    (6, "W"): (("R1", 6),),
+    (7, "F"): (("R2", 5),),
+    (7, "H"): (("R1", 7), ("R2", 6),),
+    (8, "V"): (("R2", 7),),
+    (8, "W"): (("R3", 4), ("R3", 5), ("R3", 6), ("R3", 7), ("R4", 4), ("R4", 5), ("R4", 6), ("R4", 7), ("M",
+        4), ("M", 5), ("M", 6), ("M", 7),),
+}
 
 
 def kernel(
@@ -172,46 +196,27 @@
     for peer in (to_yp, to_ym, to_zp, to_zm, to_below, to_above):
         pl.semaphore_signal(barrier, inc=1, device_id=peer, device_id_type=MESH)
 
-    lane = lax.broadcasted_iota(jnp.int32, (ROWS, 128), 1)
+    expert = lax.broadcasted_iota(jnp.int32, (OWNERS, CHUNKS * ROWS), 0)
+    halves = []
+    for m in range(2):
+        dense = jnp.zeros((OWNERS, CHUNKS * ROWS), F32)
+        for choice in range(TOPK):
+            hit = routes[choice, m:m + 1, :] == expert
+            dense = dense + jnp.where(hit, gates[choice, m:m + 1, :], 0.0)
+        halves.append(dense)
+    dense = jnp.concatenate(halves, axis=1)
+    high = dense.astype(BF16).astype(F32)
+    mid = (dense - high).astype(BF16).astype(F32)
+    low = dense - high - mid
+    blank = jnp.zeros((128 - 3 * OWNERS, STEPS * ROWS), F32)
+    packed = jnp.concatenate([high, mid, low, blank], axis=0).T.astype(BF16)
     for k in range(STEPS):
-        m, c = divmod(k, CHUNKS)
-        ids = routes[m, c * ROWS:(c + 1) * ROWS, :]
-        values = gates[m, c * ROWS:(c + 1) * ROWS, :]
-        dense = jnp.zeros((ROWS, 128), F32)
-        for choice in range(TOPK):
-            hit = ids[:, choice:choice + 1] == (lane & (OWNERS - 1))
-            dense = dense + jnp.where(hit, values[:, choice:choice + 1], 0.0)
-        high = dense.astype(BF16).astype(F32)
-        rest = dense - high
-        mid = rest.astype(BF16).astype(F32)
-        low = rest - mid
-        packed = jnp.where(
-            lane < OWNERS, high,
-            jnp.where(lane < 2 * OWNERS, mid, jnp.where(lane < 3 * OWNERS, low, 0.0)),
-        )
-        blk(cots, k, z, y, D, 128)[...] = packed.astype(BF16)
-
-    acc_g[...] = jnp.zeros_like(acc_g)
-    acc_u[...] = jnp.zeros_like(acc_u)
-    acc_d[...] = jnp.zeros_like(acc_d)
+        blk(cots, k, z, y, D, 128)[...] = packed[k * ROWS:(k + 1) * ROWS]
+
     pick_row = lax.broadcasted_iota(jnp.int32, (128, 128), 0)
     picker = jnp.where(
         ((pick_row & (OWNERS - 1)) == own) & (pick_row < 3 * OWNERS), 1.0, 0.0
     ).astype(BF16)
-
-    for c in range(CHUNKS):
-        row_load(c).wait()
-        cot_load(c).wait()
-    pl.semaphore_wait(barrier, 6)
-    ag_start(0, 0)
-    for copy in loads:
-        copy.wait()
-    for c in range(CHUNKS, STEPS):
-        row_load(c).wait()
-    ag_wait(0, 0)
-    ag_start(1, 0)
-    ag_wait(1, 0)
-    ag_start(2, 0)
 
     def forward(j):
         rows = xs[j].reshape(ALL_ROWS, D)
@@ -242,6 +247,8 @@
             hid_s[turn, :, cols] = (swished * up_value).astype(BF16)
             gg_s[turn, :, cols] = (grad_hidden * up_value * derivative).astype(BF16)
             gu_s[turn, :, cols] = (grad_hidden * swished).astype(BF16)
+    def send_back(j):
+        turn = j % 2
         for n in range(D // 256):
             cols = slice(n * 256, (n + 1) * 256)
             back = lax.dot_general(gg_s[turn], wg[cols, :], NT, preferred_element_type=F32)
@@ -264,107 +271,103 @@
                 hid_s[turn], scaled_s[turn, :, cols], TN, preferred_element_type=F32
             )
 
-    @pl.loop(0, STEPS + 2)
+    def fold_far(r):
+        add_to(zrow(part, r, zm, 0, QUART), land1z.at[r, 0])
+        add_to(zrow(part, r, zp, QUART, QUART), land1z.at[r, 1])
+        add_to(ycol(part, r, ym, HALF, QUART), land1y.at[r, 0])
+        add_to(ycol(part, r, yp, HALF + QUART, QUART), land1y.at[r, 1])
+
+    def fold_ring(r):
+        add_to(zrow(part, r, z, 0, HALF), land2z.at[r, 0], land2z.at[r, 1])
+        add_to(ycol(part, r, y, HALF, HALF), land2y.at[r, 0], land2y.at[r, 1])
+
+    def fold_corner(r):
+        add_to(blk(part, r, z, ym, 0, QUART), land3.at[r, 0])
+        add_to(blk(part, r, z, yp, QUART, QUART), land3.at[r, 1])
+        add_to(blk(part, r, zm, y, HALF, QUART), land3.at[r, 2])
+        add_to(blk(part, r, zp, y, HALF + QUART, QUART), land3.at[r, 3])
+
+    def finish(r):
+        for part_no in range(2):
+            base = part_no * HALF
+            total = blk(cots, r, z, y, base, HALF)[...].astype(F32)
+            total = total + blk(part, r, z, y, base, HALF)[...].astype(F32)
+            total = total + land4[r, part_no * 2].astype(F32)
+            total = total + land4[r, part_no * 2 + 1].astype(F32)
+            outs[r, :, base:base + HALF] = total.astype(BF16)
+        if r < CHUNKS:
+            move(r).start()
+
+    def act(kind, i):
+        phase = int(kind[1:]) - 1 if len(kind) > 1 else 4
+        if kind[0] == "P":
+            if phase == 0:
+                row_load(i).wait()
+                if i < CHUNKS:
+                    cot_load(i).wait()
+                else:
+                    c = i - CHUNKS
+                    move(c).wait_recv()
+                    top = sec == n_sec - 1
+                    value = jnp.where(top, head[at_rows(c), :], moved[c])
+                    blk(cots, i, z, y, 0, D)[...] = value
+            else:
+                ag_wait(phase - 1, i)
+            ag_start(phase, i)
+        else:
+            if phase > 0:
+                rs_wait(phase - 1, i)
+                (fold_far, fold_ring, fold_corner, finish)[phase - 1](i)
+            if phase < 4:
+                rs_start(phase, i)
+
+    stores = [
+        pltpu.make_async_copy(wg, grad_gate, load_sem.at[0]),
+        pltpu.make_async_copy(wu, grad_up, load_sem.at[1]),
+        pltpu.make_async_copy(wd, grad_down, load_sem.at[2]),
+        pltpu.make_async_copy(outs, grads, load_sem.at[3]),
+    ]
+
+    pl.semaphore_wait(barrier, 6)
+    for number, (kind, i) in enumerate(HEAD):
+        act(kind, i)
+        if number == CHUNKS:
+            acc_g[...] = jnp.zeros_like(acc_g)
+            acc_u[...] = jnp.zeros_like(acc_u)
+            acc_d[...] = jnp.zeros_like(acc_d)
+    for copy in loads:
+        copy.wait()
+
+    @pl.loop(0, STEPS + 1)
     def _(t):
-        k, j, r, n = t, t - 1, t - 2, t + 1
-        gathering = k < STEPS
-        coming = n < STEPS
-        working = (t >= 1) & (j < STEPS)
-        reducing = t >= 2
-
-        @pl.when(reducing)
-        def _():
-            rs_wait(0, r)
-            add_to(zrow(part, r, zm, 0, QUART), land1z.at[r, 0])
-            add_to(zrow(part, r, zp, QUART, QUART), land1z.at[r, 1])
-            add_to(ycol(part, r, ym, HALF, QUART), land1y.at[r, 0])
-            add_to(ycol(part, r, yp, HALF + QUART, QUART), land1y.at[r, 1])
-            rs_start(1, r)
-
-        @pl.when(working)
-        def _():
-            forward(j)
-
-        @pl.when(coming & (n >= CHUNKS))
-        def _():
-            c = n - CHUNKS
-            move(c).wait_recv()
-            top = sec == n_sec - 1
-            value = jnp.where(top, head[at_rows(c), :], moved[c])
-            blk(cots, n, z, y, 0, D)[...] = value
-
-        @pl.when(coming)
-        def _():
-            ag_start(0, n)
-
-        @pl.when(working)
-        def _():
-            backward(j)
-            rs_start(0, j)
-
-        @pl.when(gathering)
-        def _():
-            ag_wait(2, k)
-            ag_start(3, k)
-
-        @pl.when(reducing)
-        def _():
-            rs_wait(1, r)
-            add_to(zrow(part, r, z, 0, HALF), land2z.at[r, 0], land2z.at[r, 1])
-            add_to(ycol(part, r, y, HALF, HALF), land2y.at[r, 0], land2y.at[r, 1])
-            rs_start(2, r)
-            grow_up_gate(r)
-
-        @pl.when(coming)
-        def _():
-            ag_wait(0, n)
-            ag_start(1, n)
-
-        @pl.when(reducing)
-        def _():
-            rs_wait(2, r)
-            add_to(blk(part, r, z, ym, 0, QUART), land3.at[r, 0])
-            add_to(blk(part, r, z, yp, QUART, QUART), land3.at[r, 1])
-            add_to(blk(part, r, zm, y, HALF, QUART), land3.at[r, 2])
-            add_to(blk(part, r, zp, y, HALF + QUART, QUART), land3.at[r, 3])
-            rs_start(3, r)
-            grow_down(r)
-
-        @pl.when(coming)
-        def _():
-            ag_wait(1, n)
-            ag_start(2, n)
-
-        @pl.when(reducing)
-        def _():
-            rs_wait(3, r)
-            for part_no in range(2):
-                base = part_no * HALF
-                total = blk(cots, r, z, y, base, HALF)[...].astype(F32)
-                total = total + blk(part, r, z, y, base, HALF)[...].astype(F32)
-                total = total + land4[r, part_no * 2].astype(F32)
-                total = total + land4[r, part_no * 2 + 1].astype(F32)
-                outs[r, :, base:base + HALF] = total.astype(BF16)
-
-            @pl.when(r < CHUNKS)
+        def after(step):
+            for (when, name), todo in AFTER.items():
+                if name == step:
+                    @pl.when(t == when)
+                    def _():
+                        for kind, i in todo:
+                            act(kind, i)
+
+        for step, work in (("F", forward), ("G", backward), ("H", send_back)):
+            @pl.when(t < STEPS)
             def _():
-                move(r).start()
-
-        @pl.when(gathering)
-        def _():
-            ag_wait(3, k)
-
-    wg[...] = acc_g[...].astype(BF16)
-    store_g = pltpu.make_async_copy(wg, grad_gate, load_sem.at[0])
-    store_g.start()
-    wu[...] = acc_u[...].astype(BF16)
-    store_u = pltpu.make_async_copy(wu, grad_up, load_sem.at[1])
-    store_u.start()
-    wd[...] = acc_d[...].astype(BF16)
-    store_d = pltpu.make_async_copy(wd, grad_down, load_sem.at[2])
-    store_d.start()
-    store_o = pltpu.make_async_copy(outs, grads, load_sem.at[3])
-    store_o.start()
+                if step == "F":
+                    ag_wait(3, t)
+                work(t)
+            after(step)
+        for step, work in (("V", grow_up_gate), ("W", grow_down)):
+            @pl.when(t > 0)
+            def _():
+                work(t - 1)
+            if step == "W":
+                @pl.when(t == STEPS)
+                def _():
+                    for target, total, copy in zip((wg, wu, wd), (acc_g, acc_u, acc_d), stores):
+                        target[...] = total[...].astype(BF16)
+                        copy.start()
+            after(step)
+
+    stores[3].start()
 
     @pl.loop(0, STEPS)
     def _(k):
@@ -378,7 +381,7 @@
     def _(c):
         move(c).wait_send()
 
-    for copy in (store_g, store_u, store_d, store_o):
+    for copy in stores:
         copy.wait()
 
 
@@ -436,7 +439,7 @@
         cost_estimate=pl.CostEstimate(
             flops=16 * 2 * 1024 * D * FF, bytes_accessed=16 << 20, transcendentals=2 * 1024 * FF
         ),
-    )(inputs[0], routes[0], gates[0], cot_early[0], head_grad, w_gate[0, 0], w_up[0, 0], w_down[0, 0])
+    )(inputs[0], jnp.transpose(routes[0], (2, 0, 1)), jnp.transpose(gates[0], (2, 0, 1)), cot_early[0], head_grad, w_gate[0, 0], w_up[0, 0], w_down[0, 0])
     tokens = CHUNKS * ROWS
     grads = grads.reshape(2, 1, tokens, D)
     return grads[0], grads[1], grad_gate[None, None], grad_up[None, None], grad_down[None, None]

time: 195 us -> 164 us (0.84)
  Pallas kernels: 181 us -> 153 us
  local copies, waits for them, and re-layouts: 11.6 us -> 8.73 us
    pallas_call x1, Pallas kernels: 181 us -> 153 us  [on_device(): pl.pallas_call(kernel, out_shape=(shape((STEPS, ROWS, D), BF16), shape((D...]
    unnamed x9 -> x7, local copies, waits for them, and re-layouts: 9.71 us -> 6.86 us
where the time goes in v1:
time: 164 us; the launch traced here: 163 us
  Pallas kernels  153 us (93%)
  local copies, waits for them, and re-layouts  8.73 us (5%)
    pallas_call x1, Pallas kernels, on_device(): pl.pallas_call(kernel, out_shape=(shape((STEPS, ROWS, D), BF16), shape((D...  153 us
    unnamed x7, local copies, waits for them, and re-layouts  6.86 us

profile of v1, /device:TPU:0, one launch (start us, length us, event | category | flops | bytes accessed | tf_op | source)
XLA Modules:
  0.0 162.8 jit_solution(10486077502472042011)
XLA Ops:
  0.6 153.5 %shard_map.119 = (bf16[8,16,2048]{2,1,0:T(8,128)(2,1)}, bf16[2048,512]{1,0:T(8,128)(2,1)}, bf16[2048,512]{1,0:T(8,128)(2,1)}, bf16[512,2048]{1,0:T(8,128)(2,1)}) custom-call(bf16[2,64,2048]{2,1,0:T(8,128)(2,1)} %bitcast.24, s32[10,2,64]{2,1,0:T(2,128)} %bitcast.26, f32[10,2,64]{2,1,0:T(2,128)} %bitcast.27, bf16[64,2048]{1,0:T(8,128)(2,1)} %bitcast.25, ...), custom_call_target="tpu_custom_call" | custom-call | flops 34359738368 | bytes 16777216 | tf_op jit(solution)/shard_map/pallas_call | solution.py:393
  154.1 1.9 %fusion = (bf16[4,16,2048]{2,1,0:T(8,128)(2,1)}, bf16[4,16,2048]{2,1,0:T(8,128)(2,1)}) fusion(bf16[8,16,2048]{2,1,0:T(8,128)(2,1)} %get-tuple-element.9), kind=kLoop, calls=%fused_computation | loop fusion | bytes 1048576 | tf_op jit(solution)/shard_map/slice | solution.py:445
  156.0 0.0 copy-start.1
  156.0 3.2 %copy.16 = bf16[1,1,2048,512]{3,2,1,0:T(8,128)(2,1)} copy(bf16[1,1,2048,512]{3,2,1,0:T(8,128)(2,1)} %bitcast.18) | data formatting | bytes 4194304
  159.2 0.0 copy-done.1
  159.2 0.0 copy-start
  159.2 1.3 copy.17
  160.5 1.0 copy-done
  161.5 1.3 copy.18
Async XLA Ops:
  156.0 3.2 %copy-start.1 = (bf16[2048,512]{1,0:T(8,128)(2,1)S(1)}, bf16[2048,512]{1,0:T(8,128)(2,1)}, u32[]{:S(2)}) copy-start(bf16[2048,512]{1,0:T(8,128)(2,1)} %get-tuple-element.11) | copy-start | bytes 6291460
  159.2 2.3 %copy-start = (bf16[512,2048]{1,0:T(8,128)(2,1)S(1)}, bf16[512,2048]{1,0:T(8,128)(2,1)}, u32[]{:S(2)}) copy-start(bf16[512,2048]{1,0:T(8,128)(2,1)} %get-tuple-element.12) | copy-start | bytes 6291460

commit v2 on v1

--- a/solution.py
+++ b/solution.py
@@ -54,8 +54,8 @@
 
 def kernel(
     inputs, routes, gates, cot_early, head_grad, w_gate, w_up, w_down,
-    grads, grad_gate, grad_up, grad_down,
-    xs, cots, part, land1z, land1y, land2z, land2y, land3, land4, moved, outs, head,
+    early, late, grad_gate, grad_up, grad_down,
+    xs, cots, part, land1z, land1y, land2z, land2y, land3, land4, moved, head,
     wg, wu, wd, gate_s, up_s, hid_s, gg_s, gu_s, scaled_s, acc_g, acc_u, acc_d,
     load_sem, ag_send, ag_recv, rs_send, rs_recv, mv_send, mv_recv,
 ):
@@ -163,7 +163,7 @@
         ref[...] = total.astype(BF16)
 
     def move(c):
-        return remote(outs.at[c], moved.at[c], mv_send.at[c], mv_recv.at[c], to_below)
+        return remote(early.at[c], moved.at[c], mv_send.at[c], mv_recv.at[c], to_below)
 
     loads = [
         pltpu.make_async_copy(w_gate, wg, load_sem.at[0]),
@@ -294,7 +294,7 @@
             total = total + blk(part, r, z, y, base, HALF)[...].astype(F32)
             total = total + land4[r, part_no * 2].astype(F32)
             total = total + land4[r, part_no * 2 + 1].astype(F32)
-            outs[r, :, base:base + HALF] = total.astype(BF16)
+            (early, late)[r // CHUNKS][r % CHUNKS, :, base:base + HALF] = total.astype(BF16)
         if r < CHUNKS:
             move(r).start()
 
@@ -321,13 +321,6 @@
             if phase < 4:
                 rs_start(phase, i)
 
-    stores = [
-        pltpu.make_async_copy(wg, grad_gate, load_sem.at[0]),
-        pltpu.make_async_copy(wu, grad_up, load_sem.at[1]),
-        pltpu.make_async_copy(wd, grad_down, load_sem.at[2]),
-        pltpu.make_async_copy(outs, grads, load_sem.at[3]),
-    ]
-
     pl.semaphore_wait(barrier, 6)
     for number, (kind, i) in enumerate(HEAD):
         act(kind, i)
@@ -362,12 +355,9 @@
             if step == "W":
                 @pl.when(t == STEPS)
                 def _():
-                    for target, total, copy in zip((wg, wu, wd), (acc_g, acc_u, acc_d), stores):
+                    for target, total in zip((grad_gate, grad_up, grad_down), (acc_g, acc_u, acc_d)):
                         target[...] = total[...].astype(BF16)
-                        copy.start()
             after(step)
-
-    stores[3].start()
 
     @pl.loop(0, STEPS)
     def _(k):
@@ -381,7 +371,15 @@
     def _(c):
         move(c).wait_send()
 
-    for copy in stores:
+
+def store_results(*refs):
+    sources, targets, sem = refs[:5], refs[5:10], refs[10]
+    copies = [
+        pltpu.make_async_copy(src, dst, sem.at[i]) for i, (src, dst) in enumerate(zip(sources, targets))
+    ]
+    for copy in copies:
+        copy.start()
+    for copy in copies:
         copy.wait()
 
 
@@ -390,16 +388,17 @@
     vmem = pl.BlockSpec(memory_space=pltpu.VMEM)
     shape = jax.ShapeDtypeStruct
     block = SIDE * ROWS
-    grads, grad_gate, grad_up, grad_down = pl.pallas_call(
+    early, late, grad_gate, grad_up, grad_down = pl.pallas_call(
         kernel,
         out_shape=(
-            shape((STEPS, ROWS, D), BF16),
-            shape((D, FF), BF16),
-            shape((D, FF), BF16),
-            shape((FF, D), BF16),
+            pltpu.VMEM((CHUNKS, ROWS, D), BF16),
+            pltpu.VMEM((CHUNKS, ROWS, D), BF16),
+            pltpu.VMEM((D, FF), BF16),
+            pltpu.VMEM((D, FF), BF16),
+            pltpu.VMEM((FF, D), BF16),
         ),
         in_specs=[hbm, vmem, vmem, hbm, hbm, hbm, hbm, hbm],
-        out_specs=[hbm] * 4,
+        out_specs=[vmem] * 5,
         scratch_shapes=[
             pltpu.VMEM((STEPS, SIDE, block, D), BF16),
             pltpu.VMEM((STEPS, SIDE, block, WIDE), BF16),
@@ -411,7 +410,6 @@
             pltpu.VMEM((STEPS, 4, ROWS, QUART), BF16),
             pltpu.VMEM((STEPS, 4, ROWS, HALF), BF16),
             pltpu.VMEM((CHUNKS, ROWS, D), BF16),
-            pltpu.VMEM((STEPS, ROWS, D), BF16),
             pltpu.VMEM((CHUNKS * ROWS, D), BF16),
             pltpu.VMEM((D, FF), BF16),
             pltpu.VMEM((D, FF), BF16),
@@ -434,15 +432,24 @@
             pltpu.SemaphoreType.DMA((CHUNKS,)),
         ],
         compiler_params=pltpu.CompilerParams(
-            collective_id=0, has_side_effects=True, vmem_limit_bytes=67043328
+            collective_id=0, has_side_effects=True, vmem_limit_bytes=59500000
         ),
         cost_estimate=pl.CostEstimate(
             flops=16 * 2 * 1024 * D * FF, bytes_accessed=16 << 20, transcendentals=2 * 1024 * FF
         ),
     )(inputs[0], jnp.transpose(routes[0], (2, 0, 1)), jnp.transpose(gates[0], (2, 0, 1)), cot_early[0], head_grad, w_gate[0, 0], w_up[0, 0], w_down[0, 0])
-    tokens = CHUNKS * ROWS
-    grads = grads.reshape(2, 1, tokens, D)
-    return grads[0], grads[1], grad_gate[None, None], grad_up[None, None], grad_down[None, None]
+    results = (early, late, grad_gate, grad_up, grad_down)
+    early, late, grad_gate, grad_up, grad_down = pl.pallas_call(
+        store_results,
+        out_shape=tuple(shape(result.shape, BF16) for result in results),
+        in_specs=[hbm] * 5,
+        out_specs=[hbm] * 5,
+        scratch_shapes=[pltpu.SemaphoreType.DMA((5,))],
+        compiler_params=pltpu.CompilerParams(vmem_limit_bytes=1 << 20),
+    )(*results)
+    early = early.reshape(1, CHUNKS * ROWS, D)
+    late = late.reshape(1, CHUNKS * ROWS, D)
+    return early, late, grad_gate[None, None], grad_up[None, None], grad_down[None, None]
 
 
 def solution(mesh):

time: 164 us -> 158 us (0.963)
  local copies, waits for them, and re-layouts: 8.73 us -> 0 us
  Pallas kernels: 153 us -> 156 us
    unnamed x7 -> x0, local copies, waits for them, and re-layouts: 6.86 us -> none
    pallas_call x1 -> x2, Pallas kernels: 153 us -> 156 us  [the longest x1 153 us: on_device(): pl.pallas_call(kernel, out_shape=(pltpu.VMEM((CHUNKS, ROWS, D), BF16), pl...]
    slice x1 -> x0, local copies, waits for them, and re-layouts: 1.87 us -> none  [on_device(): grads[1]]
where the time goes in v2:
time: 158 us; the launch traced here: 157 us
  Pallas kernels  156 us (99%)
    pallas_call x1, Pallas kernels, on_device(): pl.pallas_call(kernel, out_shape=(pltpu.VMEM((CHUNKS, ROWS, D), BF16), pl...  153 us

profile of v2, /device:TPU:0, one launch (start us, length us, event | category | flops | bytes accessed | tf_op | source)
XLA Modules:
  0.0 156.6 jit_solution(8176354718390311019)
XLA Ops:
  0.6 153.1 %shard_map.119 = (bf16[4,16,2048]{2,1,0:T(8,128)(2,1)S(1)}, bf16[4,16,2048]{2,1,0:T(8,128)(2,1)S(1)}, bf16[2048,512]{1,0:T(8,128)(2,1)S(1)}, bf16[2048,512]{1,0:T(8,128)(2,1)S(1)}, bf16[512,2048]{1,0:T(8,128)(2,1)S(1)}) custom-call(bf16[2,64,2048]{2,1,0:T(8,128)(2,1)} %bitcast.22, s32[10,2,64]{2,1,0:T(2,128)} %bitcast.26, f32[10,2,64]{2,1,0:T(2,128)} %bitcast.27, ...), custom_call_target="tpu_custom_call" | custom-call | flops 34359738368 | bytes 16777216 | tf_op jit(solution)/shard_map/pallas_call | solution.py:391
  153.7 2.9 %shard_map.120 = (bf16[4,16,2048]{2,1,0:T(8,128)(2,1)}, bf16[4,16,2048]{2,1,0:T(8,128)(2,1)}, bf16[2048,512]{1,0:T(8,128)(2,1)}, bf16[2048,512]{1,0:T(8,128)(2,1)}, bf16[512,2048]{1,0:T(8,128)(2,1)}) custom-call(bf16[4,16,2048]{2,1,0:T(8,128)(2,1)S(1)} %get-tuple-element.15.refs_0_, bf16[4,16,2048]{2,1,0:T(8,128)(2,1)S(1)} %get-tuple-element.16.refs_1_, ...), custom_call_target="tpu_custom_call" | custom-call | tf_op jit(solution)/shard_map/pallas_call | solution.py:442

commit v3 on v2

--- a/solution.py
+++ b/solution.py
@@ -19,45 +19,48 @@
 ROWS = 16
 CHUNKS = 4
 STEPS = 2 * CHUNKS
-WIDE = D + 128
 HALF = D // 2
 QUART = D // 4
-COT_CUT = 1024
+SENT = D - D // 16
 ALL_ROWS = OWNERS * ROWS
 NT = (((1,), (1,)), ((), ()))
 TN = (((0,), (0,)), ((), ()))
-HEAD = (("P1", 0), ("P1", 1), ("P1", 2), ("P2", 0), ("P1", 3), ("P2", 1), ("P2", 2), ("P3", 0), ("P2", 3),
-        ("P3", 1), ("P4", 0), ("P3", 2), ("P4", 1),)
+HEAD = (("C1", 0), ("P1", 2), ("P1", 0), ("Z", 0), ("C2", 0), ("P1", 1), ("P1", 3), ("C3", 0), ("P2", 0),
+        ("P2", 1), ("P2", 2), ("P2", 3), ("C4", 0), ("P3", 0), ("P3", 1), ("P4", 0), ("P3", 2), ("C5", 0),
+        ("P4", 1),)
 AFTER = {
-    (0, "H"): (("P3", 3), ("P4", 2),),
-    (1, "W"): (("R1", 0), ("P4", 3),),
-    (2, "G"): (("R1", 1), ("R2", 0),),
-    (2, "W"): (("R1", 2),),
-    (3, "F"): (("R2", 1),),
-    (3, "G"): (("R3", 0),),
-    (3, "H"): (("R1", 3), ("R2", 2),),
-    (3, "W"): (("R4", 0), ("R3", 1), ("R2", 3), ("R3", 2), ("M", 0), ("R4", 1), ("P1", 4), ("R3", 3), ("R4",
-        2), ("M", 1), ("P2", 4), ("R4", 3), ("M", 2), ("P1", 5), ("P3", 4), ("M", 3), ("P2", 5), ("P1", 6),
-        ("P1", 7), ("P4", 4), ("P2", 6), ("P3", 5), ("P2", 7),),
-    (4, "H"): (("P3", 6),),
-    (4, "W"): (("P4", 5), ("P3", 7), ("P4", 6),),
-    (5, "W"): (("R1", 4), ("P4", 7),),
-    (6, "G"): (("R1", 5), ("R2", 4),),
-    (6, "W"): (("R1", 6),),
-    (7, "F"): (("R2", 5),),
+    (0, "F"): (("P3", 3), ("P4", 2),),
+    (0, "H"): (("R1", 0),),
+    (1, "W"): (("R1", 1), ("P4", 3),),
+    (2, "G"): (("R2", 0), ("R2", 1),),
+    (3, "F"): (("R3", 0),),
+    (3, "G"): (("R1", 2),),
+    (3, "H"): (("R1", 3), ("R3", 1), ("R4", 0), ("R2", 2), ("R2", 3), ("R4", 1), ("M", 0), ("R3", 2), ("P1",
+        4),),
+    (3, "V"): (("R3", 3), ("M", 1), ("R4", 2), ("P2", 4), ("R4", 3), ("P1", 5),),
+    (3, "W"): (("P3", 4), ("P2", 5), ("M", 2), ("M", 3), ("P1", 7), ("P1", 6), ("P4", 4), ("P2", 6), ("P3",
+        5),),
+    (4, "G"): (("P2", 7),),
+    (4, "H"): (("P3", 6), ("P4", 5),),
+    (4, "W"): (("P3", 7), ("P4", 6),),
+    (5, "H"): (("R1", 4),),
+    (5, "V"): (("P4", 7), ("R1", 5),),
+    (6, "F"): (("R2", 4),),
+    (6, "H"): (("R1", 6),),
+    (6, "W"): (("R2", 5),),
     (7, "H"): (("R1", 7), ("R2", 6),),
-    (8, "V"): (("R2", 7),),
-    (8, "W"): (("R3", 4), ("R3", 5), ("R3", 6), ("R3", 7), ("R4", 4), ("R4", 5), ("R4", 6), ("R4", 7), ("M",
-        4), ("M", 5), ("M", 6), ("M", 7),),
+    (8, "V"): (("R2", 7), ("R3", 4), ("R3", 5),),
+    (8, "W"): (("R3", 6), ("R3", 7), ("R4", 4), ("R4", 5), ("R4", 6), ("R4", 7), ("M", 4), ("M", 5), ("M", 6),
+        ("M", 7),),
 }
 
 
 def kernel(
-    inputs, routes, gates, cot_early, head_grad, w_gate, w_up, w_down,
+    inputs, routes_in, gates_in, cot_early, head_grad, w_gate, w_up, w_down,
     early, late, grad_gate, grad_up, grad_down,
-    xs, cots, part, land1z, land1y, land2z, land2y, land3, land4, moved, head,
+    xs, cots, part, land1z, land1y, land2z, land2y, land3, land4, moved, head, routes, gates, shares, own_gate,
     wg, wu, wd, gate_s, up_s, hid_s, gg_s, gu_s, scaled_s, acc_g, acc_u, acc_d,
-    load_sem, ag_send, ag_recv, rs_send, rs_recv, mv_send, mv_recv,
+    load_sem, ag_send, ag_recv, rs_send, rs_recv, mv_send, mv_recv, gate_send, gate_recv,
 ):
     sec = lax.axis_index("section")
     own = lax.axis_index("expert")
@@ -93,8 +96,7 @@
 
     def ag_copy(which, phase, side, k, arriving):
         buf = cots if which else xs
-        width = WIDE if which else D
-        cut = COT_CUT if which else HALF
+        width, cut = D, HALF
         late = phase >= 2
         on_y = (phase < 2) != bool(which)
         here, plus, minus = (y, yp, ym) if on_y else (z, zp, zm)
@@ -112,18 +114,37 @@
             ref = blk(buf, k, z, pos, col, wid)
         else:
             ref = blk(buf, k, pos, y, col, wid)
-        slot = phase * 2 + side
-        return remote(ref, ref, ag_send.at[k, which, slot], ag_recv.at[k, which, slot], peer)
+        return remote(ref, ref, ag_send.at[k], ag_recv.at[k, phase], peer)
+
+    def gate_copy(phase, side, arriving):
+        late = phase >= 2
+        here, plus, minus, opposite = (z, zp, zm, zo) if late else (y, yp, ym, yo)
+        peer = ((to_zp, to_zm) if late else (to_yp, to_ym))[side]
+        if phase % 2 == 0:
+            pos = (minus, plus)[side] if arriving else here
+            line = pl.ds(0, OWNERS)
+        else:
+            pos = opposite if arriving else (minus, plus)[side]
+            line = pl.ds(side * (OWNERS // 2), OWNERS // 2)
+        ref = shares.at[pos, :, line] if late else shares.at[z, pos, line]
+        return remote(ref, ref, gate_send, gate_recv.at[phase], peer)
 
     def ag_start(phase, k):
         for which in range(2):
             for side in range(2):
                 ag_copy(which, phase, side, k, False).start()
 
+    def await_bytes(ref, sem):
+        pltpu.make_async_copy(ref, ref, sem).wait()
+
     def ag_wait(phase, k):
-        for which in range(2):
-            for side in range(2):
-                ag_copy(which, phase, side, k, True).wait_recv()
+        whole = (
+            xs.at[k, 0], xs.at[k, 0, :, pl.ds(0, HALF)], xs.at[k], xs.at[k, :, :, pl.ds(0, HALF)]
+        )[phase]
+        await_bytes(whole, ag_recv.at[k, phase])
+
+    def ag_sent(k):
+        await_bytes(xs.at[pl.ds(0, 2), :, :, pl.ds(0, SENT)], ag_send.at[k])
 
     def rs_copy(phase, part_no, side, k):
         on_y = (part_no == 1) != (phase >= 2)
@@ -143,8 +164,7 @@
         else:
             src = blk(part, k, z, pos, col, wid) if on_y else blk(part, k, pos, y, col, wid)
             dst = (land3, land4)[phase - 2].at[k, part_no * 2 + side]
-        slot = phase * 4 + part_no * 2 + side
-        return remote(src, dst, rs_send.at[k, slot], rs_recv.at[k, slot], peer)
+        return remote(src, dst, rs_send.at[k], rs_recv.at[k, phase], peer)
 
     def rs_start(phase, k):
         for part_no in range(2):
@@ -152,9 +172,18 @@
                 rs_copy(phase, part_no, side, k).start()
 
     def rs_wait(phase, k):
-        for part_no in range(2):
-            for side in range(2):
-                rs_copy(phase, part_no, side, k).wait_recv()
+        whole = (
+            part.at[k, 0], part.at[k, :, :, pl.ds(0, HALF)],
+            part.at[k, 0, pl.ds(0, ROWS)], part.at[k, 0, pl.ds(0, 2 * ROWS)],
+        )[phase]
+        await_bytes(whole, rs_recv.at[k, phase])
+
+    def rs_sent(k):
+        await_bytes(part.at[k, :, :, pl.ds(0, SENT)], rs_send.at[k])
+
+    def gate_wait(phase):
+        width = (QUART, QUART // 2, D, HALF)[phase]
+        await_bytes(moved.at[0, :, pl.ds(0, width)], gate_recv.at[phase])
 
     def add_to(ref, *others):
         total = ref[...].astype(F32)
@@ -163,7 +192,7 @@
         ref[...] = total.astype(BF16)
 
     def move(c):
-        return remote(early.at[c], moved.at[c], mv_send.at[c], mv_recv.at[c], to_below)
+        return remote(early.at[c], moved.at[c], mv_send, mv_recv.at[c], to_below)
 
     loads = [
         pltpu.make_async_copy(w_gate, wg, load_sem.at[0]),
@@ -172,6 +201,11 @@
         pltpu.make_async_copy(head_grad, head, load_sem.at[3]),
     ]
 
+    gate_loads = [
+        pltpu.make_async_copy(routes_in, routes, load_sem.at[4 + STEPS + CHUNKS]),
+        pltpu.make_async_copy(gates_in, gates, load_sem.at[5 + STEPS + CHUNKS]),
+    ]
+
     def row_load(k):
         c = k % CHUNKS
         m = k // CHUNKS
@@ -184,6 +218,11 @@
             cot_early.at[pl.ds(c * ROWS, ROWS), :], blk(cots, c, z, y, 0, D), load_sem.at[4 + STEPS + c]
         )
 
+    barrier = pltpu.get_barrier_semaphore()
+    for peer in (to_yp, to_ym, to_zp, to_zm, to_below, to_above):
+        pl.semaphore_signal(barrier, inc=1, device_id=peer, device_id_type=MESH)
+    for copy in gate_loads:
+        copy.start()
     for c in range(CHUNKS):
         row_load(c).start()
         cot_load(c).start()
@@ -192,31 +231,30 @@
     for c in range(CHUNKS, STEPS):
         row_load(c).start()
 
-    barrier = pltpu.get_barrier_semaphore()
-    for peer in (to_yp, to_ym, to_zp, to_zm, to_below, to_above):
-        pl.semaphore_signal(barrier, inc=1, device_id=peer, device_id_type=MESH)
-
     expert = lax.broadcasted_iota(jnp.int32, (OWNERS, CHUNKS * ROWS), 0)
-    halves = []
-    for m in range(2):
-        dense = jnp.zeros((OWNERS, CHUNKS * ROWS), F32)
-        for choice in range(TOPK):
-            hit = routes[choice, m:m + 1, :] == expert
-            dense = dense + jnp.where(hit, gates[choice, m:m + 1, :], 0.0)
-        halves.append(dense)
-    dense = jnp.concatenate(halves, axis=1)
-    high = dense.astype(BF16).astype(F32)
-    mid = (dense - high).astype(BF16).astype(F32)
-    low = dense - high - mid
-    blank = jnp.zeros((128 - 3 * OWNERS, STEPS * ROWS), F32)
-    packed = jnp.concatenate([high, mid, low, blank], axis=0).T.astype(BF16)
-    for k in range(STEPS):
-        blk(cots, k, z, y, D, 128)[...] = packed[k * ROWS:(k + 1) * ROWS]
-
-    pick_row = lax.broadcasted_iota(jnp.int32, (128, 128), 0)
-    picker = jnp.where(
-        ((pick_row & (OWNERS - 1)) == own) & (pick_row < 3 * OWNERS), 1.0, 0.0
-    ).astype(BF16)
+
+    def pack_gates():
+        halves = []
+        for m in range(2):
+            dense = jnp.zeros((OWNERS, CHUNKS * ROWS), F32)
+            for choice in range(TOPK):
+                hit = routes[choice, m:m + 1, :] == expert
+                dense = dense + jnp.where(hit, gates[choice, m:m + 1, :], 0.0)
+            halves.append(dense)
+        shares[z, y] = jnp.concatenate(halves, axis=1)
+
+    def unpack_gates():
+        mine = lax.broadcasted_iota(jnp.int32, (OWNERS, STEPS * ROWS), 0) == own
+        lines = [
+            jnp.sum(jnp.where(mine, shares[bz, by], 0.0), axis=0, keepdims=True)
+            for bz in range(SIDE) for by in range(SIDE)
+        ]
+        lines.append(jnp.zeros((128 - OWNERS, STEPS * ROWS), F32))
+        columns = jnp.concatenate(lines, axis=0).T
+        for k in range(STEPS):
+            for source in range(OWNERS):
+                column = columns[k * ROWS:(k + 1) * ROWS, source:source + 1]
+                own_gate[k, source * ROWS:(source + 1) * ROWS, :] = jnp.broadcast_to(column, (ROWS, 128))
 
     def forward(j):
         rows = xs[j].reshape(ALL_ROWS, D)
@@ -227,13 +265,10 @@
 
     def backward(j):
         turn = j % 2
-        own_gate = jnp.dot(
-            cots[j, :, :, D:].reshape(ALL_ROWS, 128), picker, preferred_element_type=F32
-        )
         for n in range(D // 128):
             cols = slice(n * 128, (n + 1) * 128)
             tile = cots[j, :, :, cols].reshape(ALL_ROWS, 128).astype(F32)
-            scaled_s[turn, :, cols] = (own_gate * tile).astype(BF16)
+            scaled_s[turn, :, cols] = (own_gate[j] * tile).astype(BF16)
         for n in range(2):
             cols = slice(n * 256, (n + 1) * 256)
             grad_hidden = lax.dot_general(
@@ -314,20 +349,34 @@
             else:
                 ag_wait(phase - 1, i)
             ag_start(phase, i)
+        elif kind[0] == "C":
+            if phase == 0:
+                for copy in gate_loads:
+                    copy.wait()
+                pack_gates()
+            else:
+                gate_wait(phase - 1)
+            if phase == 4:
+                unpack_gates()
+            else:
+                for side in range(2):
+                    gate_copy(phase, side, False).start()
+        elif kind[0] == "Z":
+            acc_g[...] = jnp.zeros_like(acc_g)
+            acc_u[...] = jnp.zeros_like(acc_u)
+            acc_d[...] = jnp.zeros_like(acc_d)
         else:
             if phase > 0:
                 rs_wait(phase - 1, i)
                 (fold_far, fold_ring, fold_corner, finish)[phase - 1](i)
             if phase < 4:
                 rs_start(phase, i)
+            else:
+                rs_sent(i)
 
     pl.semaphore_wait(barrier, 6)
-    for number, (kind, i) in enumerate(HEAD):
+    for kind, i in HEAD:
         act(kind, i)
-        if number == CHUNKS:
-            acc_g[...] = jnp.zeros_like(acc_g)
-            acc_u[...] = jnp.zeros_like(acc_u)
-            acc_d[...] = jnp.zeros_like(acc_d)
     for copy in loads:
         copy.wait()
 
@@ -352,6 +401,8 @@
             @pl.when(t > 0)
             def _():
                 work(t - 1)
+                if step == "W":
+                    ag_sent(t - 1)
             if step == "W":
                 @pl.when(t == STEPS)
                 def _():
@@ -359,17 +410,8 @@
                         target[...] = total[...].astype(BF16)
             after(step)
 
-    @pl.loop(0, STEPS)
-    def _(k):
-        for phase in range(4):
-            for which in range(2):
-                for side in range(2):
-                    ag_copy(which, phase, side, k, False).wait_send()
-                    rs_copy(phase, which, side, k).wait_send()
-
-    @pl.loop(0, CHUNKS)
-    def _(c):
-        move(c).wait_send()
+    await_bytes(moved, mv_send)
+    await_bytes(part.at[0, 0, pl.ds(0, 2 * ROWS), pl.ds(0, SENT)], gate_send)
 
 
 def store_results(*refs):
@@ -397,11 +439,11 @@
             pltpu.VMEM((D, FF), BF16),
             pltpu.VMEM((FF, D), BF16),
         ),
-        in_specs=[hbm, vmem, vmem, hbm, hbm, hbm, hbm, hbm],
+        in_specs=[hbm] * 8,
         out_specs=[vmem] * 5,
         scratch_shapes=[
             pltpu.VMEM((STEPS, SIDE, block, D), BF16),
-            pltpu.VMEM((STEPS, SIDE, block, WIDE), BF16),
+            pltpu.VMEM((STEPS, SIDE, block, D), BF16),
             pltpu.VMEM((STEPS, SIDE, block, D), BF16),
             pltpu.VMEM((STEPS, 2, block, QUART), BF16),
             pltpu.VMEM((STEPS, 2, SIDE, ROWS, QUART), BF16),
@@ -411,6 +453,10 @@
             pltpu.VMEM((STEPS, 4, ROWS, HALF), BF16),
             pltpu.VMEM((CHUNKS, ROWS, D), BF16),
             pltpu.VMEM((CHUNKS * ROWS, D), BF16),
+            pltpu.VMEM((TOPK, 2, CHUNKS * ROWS), jnp.int32),
+            pltpu.VMEM((TOPK, 2, CHUNKS * ROWS), F32),
+            pltpu.VMEM((SIDE, SIDE, OWNERS, STEPS * ROWS), F32),
+            pltpu.VMEM((STEPS, ALL_ROWS, 128), F32),
             pltpu.VMEM((D, FF), BF16),
             pltpu.VMEM((D, FF), BF16),
             pltpu.VMEM((FF, D), BF16),
@@ -423,13 +469,15 @@
             pltpu.VMEM((D, FF), F32),
             pltpu.VMEM((D, FF), F32),
             pltpu.VMEM((FF, D), F32),
-            pltpu.SemaphoreType.DMA((4 + STEPS + CHUNKS,)),
-            pltpu.SemaphoreType.DMA((STEPS, 2, 8)),
-            pltpu.SemaphoreType.DMA((STEPS, 2, 8)),
-            pltpu.SemaphoreType.DMA((STEPS, 16)),
-            pltpu.SemaphoreType.DMA((STEPS, 16)),
+            pltpu.SemaphoreType.DMA((6 + STEPS + CHUNKS,)),
+            pltpu.SemaphoreType.DMA((STEPS,)),
+            pltpu.SemaphoreType.DMA((STEPS, 4)),
+            pltpu.SemaphoreType.DMA((STEPS,)),
+            pltpu.SemaphoreType.DMA((STEPS, 4)),
+            pltpu.SemaphoreType.DMA,
             pltpu.SemaphoreType.DMA((CHUNKS,)),
-            pltpu.SemaphoreType.DMA((CHUNKS,)),
+            pltpu.SemaphoreType.DMA,
+            pltpu.SemaphoreType.DMA((4,)),
         ],
         compiler_params=pltpu.CompilerParams(
             collective_id=0, has_side_effects=True, vmem_limit_bytes=59500000

time: 158 us -> 148 us (0.937)
  Pallas kernels: 156 us -> 147 us
    pallas_call x1, Pallas kernels: 153 us -> 144 us  [on_device(): pl.pallas_call(kernel, out_shape=(pltpu.VMEM((CHUNKS, ROWS, D), BF16), pl...]
where the time goes in v3:
time: 148 us
  Pallas kernels  147 us (99%)
    pallas_call x1, Pallas kernels, on_device(): pl.pallas_call(kernel, out_shape=(pltpu.VMEM((CHUNKS, ROWS, D), BF16), pl...  144 us

profile of v3, /device:TPU:0, one launch (start us, length us, event | category | flops | bytes accessed | tf_op | source)
XLA Modules:
  0.0 147.9 jit_solution(17104043717837125327)
XLA Ops:
  0.6 144.4 %shard_map.119 = (bf16[4,16,2048]{2,1,0:T(8,128)(2,1)S(1)}, bf16[4,16,2048]{2,1,0:T(8,128)(2,1)S(1)}, bf16[2048,512]{1,0:T(8,128)(2,1)S(1)}, bf16[2048,512]{1,0:T(8,128)(2,1)S(1)}, bf16[512,2048]{1,0:T(8,128)(2,1)S(1)}) custom-call(bf16[2,64,2048]{2,1,0:T(8,128)(2,1)} %bitcast.22, s32[10,2,64]{2,1,0:T(2,128)} %bitcast.26, f32[10,2,64]{2,1,0:T(2,128)} %bitcast.27, ...), custom_call_target="tpu_custom_call" | custom-call | flops 34359738368 | bytes 16777216 | tf_op jit(solution)/shard_map/pallas_call | solution.py:433
  145.0 2.9 %shard_map.120 = (bf16[4,16,2048]{2,1,0:T(8,128)(2,1)}, bf16[4,16,2048]{2,1,0:T(8,128)(2,1)}, bf16[2048,512]{1,0:T(8,128)(2,1)}, bf16[2048,512]{1,0:T(8,128)(2,1)}, bf16[512,2048]{1,0:T(8,128)(2,1)}) custom-call(bf16[4,16,2048]{2,1,0:T(8,128)(2,1)S(1)} %get-tuple-element.15.refs_0_, bf16[4,16,2048]{2,1,0:T(8,128)(2,1)S(1)} %get-tuple-element.16.refs_1_, ...), custom_call_target="tpu_custom_call" | custom-call | tf_op jit(solution)/shard_map/pallas_call | solution.py:490

commit v4 on v3

--- a/solution.py
+++ b/solution.py
@@ -25,9 +25,11 @@
 ALL_ROWS = OWNERS * ROWS
 NT = (((1,), (1,)), ((), ()))
 TN = (((0,), (0,)), ((), ()))
-HEAD = (("C1", 0), ("P1", 2), ("P1", 0), ("Z", 0), ("C2", 0), ("P1", 1), ("P1", 3), ("C3", 0), ("P2", 0),
-        ("P2", 1), ("P2", 2), ("P2", 3), ("C4", 0), ("P3", 0), ("P3", 1), ("P4", 0), ("P3", 2), ("C5", 0),
-        ("P4", 1),)
+HEAD = (
+    ("C1", 0), ("P1", 2), ("P1", 0), ("P1", 1), ("Z", 0), ("C2", 0), ("P1", 3), ("P2", 0),
+    ("C3", 0), ("P2", 1), ("P2", 2), ("P2", 3), ("P3", 0), ("C4", 0), ("P3", 1), ("P4", 0),
+    ("P3", 2), ("C5", 0), ("P4", 1),
+)
 AFTER = {
     (0, "F"): (("P3", 3), ("P4", 2),),
     (0, "H"): (("R1", 0),),
@@ -94,6 +96,10 @@
             device_id=peer, device_id_type=MESH,
         )
 
+    def own_source(which, k):
+        rows = pl.ds(k % CHUNKS * ROWS, ROWS)
+        return cot_early.at[rows] if which else inputs.at[k // CHUNKS, rows]
+
     def ag_copy(which, phase, side, k, arriving):
         buf = cots if which else xs
         width, cut = D, HALF
@@ -114,7 +120,9 @@
             ref = blk(buf, k, z, pos, col, wid)
         else:
             ref = blk(buf, k, pos, y, col, wid)
-        return remote(ref, ref, ag_send.at[k], ag_recv.at[k, phase], peer)
+        direct = phase == 0 and isinstance(k, int) and k < CHUNKS
+        src = own_source(which, k) if direct else ref
+        return remote(src, ref, ag_send.at[k], ag_recv.at[k, phase], peer)
 
     def gate_copy(phase, side, arriving):
         late = phase >= 2
@@ -207,15 +215,11 @@
     ]
 
     def row_load(k):
-        c = k % CHUNKS
-        m = k // CHUNKS
-        return pltpu.make_async_copy(
-            inputs.at[m, pl.ds(c * ROWS, ROWS), :], blk(xs, k, z, y, 0, D), load_sem.at[4 + k]
-        )
+        return pltpu.make_async_copy(own_source(0, k), blk(xs, k, z, y, 0, D), load_sem.at[4 + k])
 
     def cot_load(c):
         return pltpu.make_async_copy(
-            cot_early.at[pl.ds(c * ROWS, ROWS), :], blk(cots, c, z, y, 0, D), load_sem.at[4 + STEPS + c]
+            own_source(1, c), blk(cots, c, z, y, 0, D), load_sem.at[4 + STEPS + c]
         )
 
     barrier = pltpu.get_barrier_semaphore()
@@ -337,16 +341,17 @@
         phase = int(kind[1:]) - 1 if len(kind) > 1 else 4
         if kind[0] == "P":
             if phase == 0:
-                row_load(i).wait()
-                if i < CHUNKS:
-                    cot_load(i).wait()
-                else:
+                if i >= CHUNKS:
+                    row_load(i).wait()
                     c = i - CHUNKS
                     move(c).wait_recv()
                     top = sec == n_sec - 1
                     value = jnp.where(top, head[at_rows(c), :], moved[c])
                     blk(cots, i, z, y, 0, D)[...] = value
             else:
+                if phase == 2 and i < CHUNKS:
+                    row_load(i).wait()
+                    cot_load(i).wait()
                 ag_wait(phase - 1, i)
             ag_start(phase, i)
         elif kind[0] == "C":

time: 148 us -> 148 us (level)
  no operation moved by 1% of the time
where the time goes in v4:
time: 148 us
  Pallas kernels  147 us (99%)
    pallas_call x1, Pallas kernels, on_device(): pl.pallas_call(kernel, out_shape=(pltpu.VMEM((CHUNKS, ROWS, D), BF16), pl...  144 us

profile of v4, /device:TPU:0, one launch (start us, length us, event | category | flops | bytes accessed | tf_op | source)
XLA Modules:
  0.0 147.6 jit_solution(13381775914779717837)
XLA Ops:
  0.6 144.1 %shard_map.119 = (bf16[4,16,2048]{2,1,0:T(8,128)(2,1)S(1)}, bf16[4,16,2048]{2,1,0:T(8,128)(2,1)S(1)}, bf16[2048,512]{1,0:T(8,128)(2,1)S(1)}, bf16[2048,512]{1,0:T(8,128)(2,1)S(1)}, bf16[512,2048]{1,0:T(8,128)(2,1)S(1)}) custom-call(bf16[2,64,2048]{2,1,0:T(8,128)(2,1)} %bitcast.22, s32[10,2,64]{2,1,0:T(2,128)} %bitcast.26, f32[10,2,64]{2,1,0:T(2,128)} %bitcast.27, ...), custom_call_target="tpu_custom_call" | custom-call | flops 34359738368 | bytes 16777216 | tf_op jit(solution)/shard_map/pallas_call | solution.py:438
  144.7 2.9 %shard_map.120 = (bf16[4,16,2048]{2,1,0:T(8,128)(2,1)}, bf16[4,16,2048]{2,1,0:T(8,128)(2,1)}, bf16[2048,512]{1,0:T(8,128)(2,1)}, bf16[2048,512]{1,0:T(8,128)(2,1)}, bf16[512,2048]{1,0:T(8,128)(2,1)}) custom-call(bf16[4,16,2048]{2,1,0:T(8,128)(2,1)S(1)} %get-tuple-element.15.refs_0_, bf16[4,16,2048]{2,1,0:T(8,128)(2,1)S(1)} %get-tuple-element.16.refs_1_, ...), custom_call_target="tpu_custom_call" | custom-call | tf_op jit(solution)/shard_map/pallas_call | solution.py:495
